TPU v7x, 256 devices: a whole 4x4x8 slice. The times are simulated.
256 devices in a mesh: gx: 16 (over x, y_lo, core), gy: 16 (over y_hi, z).
Axes of the slice: x: 4, y: 4 (y_hi: 2, y_lo: 2; y = y_hi * 2 + y_lo), z: 8, core: 2. Of those that a mesh axis runs over, the one named last changes fastest.
Arguments:
- object_field: float32 [2, 1024, 1024], P(None, 'gy', 'gx'), may hold values from -1 to 1
- probe_modes: float32 [2, 1024, 128], P(None, ('gy', 'gx')), may hold values from -1.5 to 1.5
- positions: int32 [16, 16, 12, 2], P('gy', 'gx'), may hold values from 4 to 60, as said below
- amplitudes: float32 [16, 16, 12, 128, 128], P('gy', 'gx'), may hold values from 0 to 2
Outputs:
- object_out: float32 [2, 1024, 1024], P(None, 'gy', 'gx')
- probe_out: float32 [2, 1024, 128], P(None, ('gy', 'gx'))
Inputs may be any that keep to these rules, and one draw needn't show every extreme that they name: `positions`: each entry is a (row, column) inside its own tile; the centres of one tile lie at distinct cells of the 16 grid, each moved from the cell's middle by at most 4 cells along each dimension.
All inputs are finite; a program needn't handle non-finite values.
Results may differ from a plain program's by a relative error of at most 0.00065.
The roundings to bfloat16 on the way count: a program that leaves them out, or rounds other values in their place, can miss the bound.
Values sent between devices are 32-bit elements; how exact they have to be, the bound alone decides.
No kernel may reach another device: no remote copies, remote signals or barrier semaphores. Data moves between devices by JAX's collectives and lax.ppermute only.
A program may use at most 64 MiB of HBM per device.

v0:
```python
import math
import jax
import jax.numpy as jnp
from jax import lax
from jax.sharding import PartitionSpec as P

MODES = 8
ITERS = 2
SOFT_FLOOR = 0.05
OBJECT_REG = 1.0
PROBE_REG = 1.0


def from_behind(block, axis, distance):
    devices = range(lax.axis_size(axis))
    route = [(i - distance, i) for i in devices if i - distance in devices]
    return lax.ppermute(block, axis, route)


def extended_2(array, sides, width):
    for axis, dim in sides:
        peers, length = (lax.axis_size(axis), array.shape[dim])
        up = [(i, (i + 1) % peers) for i in range(peers - 1)]
        down = [(j, i) for i, j in up]
        last = lax.slice_in_dim(array, length - width, length, axis=dim)
        initial = lax.slice_in_dim(array, 0, width, axis=dim)
        before = lax.ppermute(last, axis, up)
        after = lax.ppermute(initial, axis, down)
        array = jnp.concatenate([before, array, after], axis=dim)
    return array


def tables(probe_side, sign_flip):
    indices = jnp.arange(probe_side, dtype=jnp.int32)
    phases = indices[:, None] * indices[None, :] % probe_side
    angles = phases.astype(jnp.float32) * (2.0 * math.pi / probe_side)
    factor = 1.0 / math.sqrt(probe_side)
    cosine = jnp.cos(angles) * factor
    sine_part = sign_flip * jnp.sin(angles) * factor
    left_op = jnp.stack(
        [jnp.stack([cosine, -sine_part]), jnp.stack([sine_part, cosine])]
    ).transpose(0, 2, 1, 3)
    right_op = jnp.stack(
        [jnp.stack([cosine, sine_part]), jnp.stack([-sine_part, cosine])]
    ).transpose(0, 2, 1, 3)
    return (left_op.astype(jnp.bfloat16), right_op.astype(jnp.bfloat16))


def transform(signal, operators):
    left_op, right_op = operators
    halfway = jnp.einsum(
        "dpcr,crmq->dpmq", left_op, signal, preferred_element_type=jnp.float32
    ).astype(jnp.bfloat16)
    return jnp.einsum("crmq,cqdk->drmk", halfway, right_op, preferred_element_type=jnp.float32)


def position_terms(patch_obj, probe, measured, forward, inverse):
    obj_real = patch_obj[0][:, None, :]
    obj_imag = patch_obj[1][:, None, :]
    wave_real = probe[0] * obj_real - probe[1] * obj_imag
    wave_imag = probe[0] * obj_imag + probe[1] * obj_real
    signal = jnp.stack([wave_real, wave_imag]).astype(jnp.bfloat16)
    spectrum = transform(signal, forward)
    intensity = jnp.sum(spectrum[0] * spectrum[0] + spectrum[1] * spectrum[1], axis=1)
    shrink = 1.0 - measured / jnp.sqrt(intensity + SOFT_FLOOR)
    residual = (spectrum * shrink[None, :, None, :]).astype(jnp.bfloat16)
    change = transform(residual, inverse)
    grad_real = jnp.sum(probe[0] * change[0] + probe[1] * change[1], axis=1)
    grad_imag = jnp.sum(probe[0] * change[1] - probe[1] * change[0], axis=1)
    probe_real = obj_real * change[0] + obj_imag * change[1]
    probe_imag = obj_real * change[1] - obj_imag * change[0]
    weight_probe = patch_obj[0] * patch_obj[0] + patch_obj[1] * patch_obj[1]
    return (jnp.stack([grad_real, grad_imag]), jnp.stack([probe_real, probe_imag]), weight_probe)


def fold_rows(gradient, margin, tile_side):
    extent = gradient.shape[1]
    for direction in (1, -1):
        rim_part = gradient[:, extent - margin :, :] if direction == 1 else gradient[:, :margin, :]
        offset = margin if direction == 1 else tile_side
        arrived = from_behind(rim_part, "gy", direction)
        gradient = gradient.at[:, offset : offset + margin, :].add(arrived)
    return gradient[:, margin : margin + tile_side, :]


def fold_cols(gradient, margin, tile_side):
    extent = gradient.shape[2]
    for direction in (1, -1):
        rim_part = gradient[:, :, extent - margin :] if direction == 1 else gradient[:, :, :margin]
        offset = margin if direction == 1 else tile_side
        arrived = from_behind(rim_part, "gx", direction)
        gradient = gradient.at[:, :, offset : offset + margin].add(arrived)
    return gradient[:, :, margin : margin + tile_side]


def unpack_probe(probe_rows, probe_side):
    return probe_rows.reshape(2, MODES, probe_side, probe_side).transpose(0, 2, 1, 3)


def local(object_field, probe_modes, positions, amplitudes):
    probe_side = amplitudes.shape[-1]
    margin = probe_side // 2
    tile_side = object_field.shape[1]
    centres = positions.reshape(-1, 2)
    measured_all = amplitudes.reshape(-1, probe_side, probe_side)
    forward = tables(probe_side, -1.0)
    inverse = tables(probe_side, 1.0)
    gathered = lax.all_gather(probe_modes, ("gy", "gx"), axis=1, tiled=True)
    probe = unpack_probe(gathered, probe_side)
    own_rows = probe_modes
    current = object_field
    for iteration in range(ITERS):
        extended = extended_2(current, (("gy", 1), ("gx", 2)), margin)
        weight_obj = jnp.sum(probe[0] * probe[0] + probe[1] * probe[1], axis=1)

        def visit(running, visit_item):
            grad_obj, grad_probe, weight_probe = running
            row_at, col_at, measured = visit_item
            zero_index = jnp.int32(0)
            patch_obj = lax.dynamic_slice(
                extended, (zero_index, row_at, col_at), (2, probe_side, probe_side)
            )
            g_obj, g_probe, w_probe = position_terms(patch_obj, probe, measured, forward, inverse)
            stacked = jnp.concatenate([g_obj, weight_obj[None]], axis=0)
            before = lax.dynamic_slice(
                grad_obj, (zero_index, row_at, col_at), (3, probe_side, probe_side)
            )
            grad_obj = lax.dynamic_update_slice(
                grad_obj, before + stacked, (zero_index, row_at, col_at)
            )
            return ((grad_obj, grad_probe + g_probe, weight_probe + w_probe), None)

        initial = (
            jnp.zeros((3, tile_side + probe_side, tile_side + probe_side), jnp.float32),
            jnp.zeros((2, probe_side, MODES, probe_side), jnp.float32),
            jnp.zeros((probe_side, probe_side), jnp.float32),
        )
        (grad_obj, grad_probe, weight_probe), _ = lax.scan(
            visit, initial, (centres[:, 0], centres[:, 1], measured_all)
        )
        folded = fold_cols(fold_rows(grad_obj, margin, tile_side), margin, tile_side)
        new_object = current - folded[0:2] / (folded[2] + OBJECT_REG)
        grad_rows = grad_probe.transpose(0, 2, 1, 3).reshape(2, MODES * probe_side, probe_side)
        totals, weight_total = lax.psum((grad_rows, weight_probe), ("gy", "gx"))
        whole_probe = probe.transpose(0, 2, 1, 3)
        whole_probe = whole_probe - totals.reshape(2, MODES, probe_side, probe_side) / (
            weight_total[None, None] + PROBE_REG
        )
        whole_probe = whole_probe.reshape(2, MODES * probe_side, probe_side)
        probe = unpack_probe(whole_probe, probe_side)
        row_count = own_rows.shape[1]
        own_rows = lax.dynamic_slice_in_dim(
            whole_probe, lax.axis_index(("gy", "gx")) * row_count, row_count, 1
        )
        current = new_object
    return (current, own_rows)


def solution(mesh):
    return jax.shard_map(
        local,
        mesh=mesh,
        in_specs=(
            P(None, "gy", "gx"),
            P(None, ("gy", "gx"), None),
            P("gy", "gx", None, None),
            P("gy", "gx", None, None, None),
        ),
        out_specs=(P(None, "gy", "gx"), P(None, ("gy", "gx"), None)),
        check_vma=False,
    )
```

profile of v0, /device:TPU:16, one launch (start us, length us, event | category | flops | bytes accessed | tf_op | source)
XLA Modules:
  0.0 1355.4 jit_solution(5158283582343708737)
XLA Ops:
  8.6 3.8 collective-permute-start
  12.4 5.6 collective-permute-start.1
  24.8 3.6 collective-permute-done.3
  29.3 362.2 %all-gather.2.cloned.1.call-done = f32[2,1024,128]{2,0,1:T(2,128)} async-done(((f32[2,4,128]{2,0,1:T(2,128)}), f32[2,1024,128]{2,0,1:T(2,128)}) %all-gather.2.cloned.1.call-update) | async-done | bytes 1048592 | tf_op jit(solution)/shard_map/all_gather | solution.py:108
  394.4 205.2 %while.38 = (s32[]{:T(128)}, f32[3,192,192]{2,1,0:T(8,128)}, f32[2,128,8,128]{3,1,0,2:T(8,128)}, f32[128,128]{1,0:T(8,128)}, s32[12]{0:T(128)S(1)}, /*index=5*/s...) while((s32[]{:T(128)}, f32[3,192,192]{2,1,0:T(8,128)}, ...), condition=%wide.region_5.6_spmd.clone, body=%wide.region_1.5_spmd.clone.sunk | while | flops 543391744 | bytes 27918840 | solution.py:138
  407.9 2.7 dynamic_update_slice.10
  424.9 2.8 dynamic_update_slice.10
  442.0 2.8 dynamic_update_slice.10
  450.7 1.8 select_add_fusion.4
  459.2 2.8 dynamic_update_slice.10
  476.2 2.7 dynamic_update_slice.10
  484.8 1.8 select_add_fusion.4
  493.3 2.8 dynamic_update_slice.10
  502.0 1.8 select_add_fusion.4
  510.4 2.8 dynamic_update_slice.10
  519.1 1.8 select_add_fusion.4
  527.6 2.8 dynamic_update_slice.10
  544.6 2.8 dynamic_update_slice.10
  561.8 2.7 dynamic_update_slice.10
  578.8 2.9 dynamic_update_slice.10
  596.0 2.8 dynamic_update_slice.10
  600.7 2.8 collective-permute-start.4
  603.5 6.7 collective-permute-start.5
  610.2 3.1 collective-permute-done.4
  618.1 1.8 copy.24
  621.1 1.9 collective-permute-start.8
  623.0 7.7 collective-permute-start.9
  632.6 4.0 collective-permute-start.10
  637.9 3.2 collective-permute-done.11
  642.1 236.9 %all-reduce.7.cloned.1.call-done = (f32[2,1024,128]{2,0,1:T(2,128)}, f32[128,128]{1,0:T(8,128)}) async-done(((f32[2,1024,128]{2,0,1:T(2,128)}, f32[128,128]{1,0:T(8,128)}), (f32[2,1024,128]{2,0,1:T(2,128)}, f32[128,128]{1,0:T(8,128)})) %all-reduce.7.cloned.1.call-update) | async-done | bytes 1114128 | tf_op jit(solution)/shard_map/psum | solution.py:144
  882.9 197.0 %while.39 = (s32[]{:T(128)}, f32[3,192,192]{2,1,0:T(8,128)}, f32[2,128,8,128]{3,1,0,2:T(8,128)}, f32[128,128]{1,0:T(8,128)}, s32[12]{0:T(128)S(1)}, /*index=5*/s...) while((s32[]{:T(128)}, f32[3,192,192]{2,1,0:T(8,128)}, ...), condition=%wide.region_13.14_spmd.clone, body=%wide.region_9.13_spmd.clone.sunk | while | flops 543391744 | bytes 27918840 | solution.py:138
  895.7 2.7 dynamic_update_slice.11
  912.0 2.8 dynamic_update_slice.11
  928.4 2.8 dynamic_update_slice.11
  944.9 2.8 dynamic_update_slice.11
  961.3 2.7 dynamic_update_slice.11
  977.7 2.8 dynamic_update_slice.11
  994.2 2.8 dynamic_update_slice.11
  1010.6 2.8 dynamic_update_slice.11
  1027.0 2.8 dynamic_update_slice.11
  1043.4 2.7 dynamic_update_slice.11
  1059.8 2.9 dynamic_update_slice.11
  1076.3 2.8 dynamic_update_slice.11
  1081.0 1.9 collective-permute-start.12
  1082.9 7.5 collective-permute-start.13
  1090.4 3.0 copy.30
  1097.3 3.0 collective-permute-done.15
  1101.9 244.8 %all-reduce.5.cloned.1.call-done = (f32[2,1024,128]{2,0,1:T(2,128)}, f32[128,128]{1,0:T(8,128)}) async-done(((f32[2,1024,128]{2,0,1:T(2,128)}, f32[128,128]{1,0:T(8,128)}), (f32[2,1024,128]{2,0,1:T(2,128)}, f32[128,128]{1,0:T(8,128)})) %all-reduce.5.cloned.1.call-update) | async-done | bytes 1114128 | tf_op jit(solution)/shard_map/psum | solution.py:144
  (689 shorter events, 276.0 us)
Async XLA Ops:
  7.2 384.3 %all-gather.2.cloned.1.call-start = ((), (), s32[]{:S(2)}) async-start(), calls=%async_computation | async-start | bytes 1052672 | tf_op jit(solution)/shard_map/all_gather | solution.py:108
  8.5 870.5 %all-reduce.7.cloned.1.call-start = ((), (), s32[]{:S(2)}) async-start(), calls=%async_computation.2 | async-start | bytes 2228224 | tf_op jit(solution)/shard_map/psum | solution.py:144
  8.6 11.9 collective-permute-start
  12.4 8.9 collective-permute-start.1
  21.4 3.5 collective-permute-start.2
  22.8 5.6 collective-permute-start.3
  407.0 3.6 copy-start.1
  424.1 3.6 copy-start.1
  441.2 3.7 copy-start.1
  458.3 3.6 copy-start.1
  475.4 3.6 copy-start.1
  492.4 3.7 copy-start.1
  509.6 3.6 copy-start.1
  526.7 3.6 copy-start.1
  543.8 3.7 copy-start.1
  560.9 3.5 copy-start.1
  577.9 3.7 copy-start.1
  595.1 3.7 copy-start.1
  599.6 18.5 %copy-start.2 = (f32[2,128,8,128]{3,1,0,2:T(8,128)S(1)}, f32[2,128,8,128]{3,1,0,2:T(8,128)}, u32[]{:S(2)}) copy-start(f32[2,128,8,128]{3,1,0,2:T(8,128)} %get-tuple-element.247) | copy-start | bytes 3145732
  600.7 12.5 collective-permute-start.4
  603.5 10.9 collective-permute-start.5
  615.5 4.5 collective-permute-start.6
  616.8 4.2 collective-permute-start.7
  619.9 260.0 %copy-start.13 = (f32[2,1024,128]{2,0,1:T(2,128)S(1)}, f32[2,1024,128]{2,0,1:T(2,128)}, u32[]{:S(2)}) copy-start(f32[2,1024,128]{2,0,1:T(2,128)} %all-gather.2.cloned.1.call-done) | copy-start | bytes 3145732
  619.9 726.8 %all-reduce.5.cloned.1.call-start = ((), (), s32[]{:S(2)}) async-start(), calls=%async_computation.1 | async-start | bytes 2228224 | tf_op jit(solution)/shard_map/psum | solution.py:144
  621.1 20.1 %copy-start.16 = (f32[2,64,64]{2,1,0:T(8,128)}, f32[2,64,64]{2,1,0:T(8,128)S(1)}, u32[]{:S(2)}) copy-start(f32[2,64,64]{2,1,0:T(8,128)S(1)} %fusion.68) | copy-start | bytes 98308
  621.1 9.9 collective-permute-start.8
  623.0 9.6 collective-permute-start.9
  632.6 5.3 collective-permute-start.10
  636.6 4.5 collective-permute-start.11
  879.9 1.4 copy-start.18
  894.8 3.6 copy-start.4
  911.2 3.6 copy-start.4
  927.6 3.7 copy-start.4
  944.1 3.6 copy-start.4
  960.5 3.6 copy-start.4
  976.8 3.7 copy-start.4
  993.3 3.6 copy-start.4
  1009.7 3.6 copy-start.4
  1026.1 3.7 copy-start.4
  1042.6 3.5 copy-start.4
  1058.9 3.7 copy-start.4
  1075.4 3.7 copy-start.4
  1081.0 12.5 collective-permute-start.12
  1082.9 10.7 collective-permute-start.13
  1094.6 2.6 copy-start.19
  1094.6 2.7 collective-permute-start.14
  1095.9 4.4 collective-permute-start.15
  (148 other events, 135.9 us)
Sparse Core Ops, SparseCore 0:
  10.4 381.0 all-gather.1
  620.0 258.9 all-reduce.6
  1093.6 253.0 all-reduce.4
where the time goes:
time: 1360 us
  waiting for transfers between devices  861 us (63%)
  local copies, waits for them, and re-layouts  158 us (12%)
  other arithmetic  136 us (10%)
  loops' own time  88.1 us (6%)
  starting transfers between devices  51.3 us (4%)
  matrix products  46.9 us (3%)
  between operations  14.2 us (1%)
    psum x2, waiting for transfers between devices, local(): totals, weight_total = lax.psum((grad_rows, weight_probe), ('gy', 'gx'))  482 us
    all_gather x1, waiting for transfers between devices, local(): gathered = lax.all_gather(probe_modes, ('gy', 'gx'), axis=1, tiled=True)  362 us
    another operation x2, loops' own time, local(): lax.scan(visit, initial, (centres[:, 0], centres[:, 1], measured_all))  88.1 us
    dynamic_update_slice x24, local copies, waits for them, and re-layouts, visit(): lax.dynamic_update_slice(grad_obj, before + stacked, (zero_index, row_at,...  66.4 us
    add x48, other arithmetic, visit(): return ((grad_obj, grad_probe + g_probe, weight_probe + w_probe), None)  50.6 us
    while x336, local copies, waits for them, and re-layouts  49.5 us
    dot_general x48, matrix products, transform(): jnp.einsum('crmq,cqdk->drmk', halfway, right_op, preferred_element_type=j...  46.9 us
    sub x24, other arithmetic, position_terms(): shrink = 1.0 - measured / jnp.sqrt(intensity + SOFT_FLOOR)  35.8 us
  transfers between devices with their start and end apart: 19, of which 12 were waited for; matrix products, arithmetic and copies ran while one was open for 1% of the time, Pallas kernels for 0%

commit v1 on v0

--- a/solution.py
+++ b/solution.py
@@ -105,7 +105,15 @@
     measured_all = amplitudes.reshape(-1, probe_side, probe_side)
     forward = tables(probe_side, -1.0)
     inverse = tables(probe_side, 1.0)
-    gathered = lax.all_gather(probe_modes, ("gy", "gx"), axis=1, tiled=True)
+    gathered = jnp.concatenate(
+        lax.all_to_all(
+            jnp.stack([probe_modes for _ in range(lax.psum(1, ("gy", "gx")))], axis=0),
+            ("gy", "gx"),
+            0,
+            0,
+        ),
+        axis=1,
+    )
     probe = unpack_probe(gathered, probe_side)
     own_rows = probe_modes
     current = object_field

time: 1360 us -> 1080 us (0.79)
  waiting for transfers between devices: 861 us -> 515 us
  local copies, waits for them, and re-layouts: 158 us -> 198 us
  starting transfers between devices: 51.3 us -> 68.8 us
    all_gather x1 -> x0, waiting for transfers between devices: 362 us -> none  [local(): gathered = lax.all_gather(probe_modes, ('gy', 'gx'), axis=1, tiled=True)]
    dynamic_slice x0 -> x48, local copies, waits for them, and re-layouts: none -> 22 us  [visit(): lax.dynamic_slice(grad_obj, (zero_index, row_at, col_at), (3, probe_side,...]
    dynamic_update_slice x24 -> x48, local copies, waits for them, and re-layouts: 66.4 us -> 82.3 us  [visit(): lax.dynamic_update_slice(grad_obj, before + stacked, (zero_index, row_at,...]
    while x336 -> x312, local copies, waits for them, and re-layouts: 49.5 us -> 34.1 us
    ppermute x4, waiting for transfers between devices: 0.31 us -> 15.5 us  [extended_2(): before = lax.ppermute(last, axis, up)]
    all_to_all x0 -> x1, starting transfers between devices: none -> 14.5 us  [local(): lax.all_to_all(jnp.stack([probe_modes for _ in range(lax.psum(1, ('gy', '...]
where the time goes in v1:
time: 1080 us; the launch traced here: 1070 us
  waiting for transfers between devices  515 us (48%)
  local copies, waits for them, and re-layouts  198 us (18%)
  other arithmetic  128 us (12%)
  loops' own time  92.6 us (9%)
  starting transfers between devices  68.8 us (6%)
  matrix products  54.9 us (5%)
  between operations  14.5 us (1%)
    psum x2, waiting for transfers between devices, local(): totals, weight_total = lax.psum((grad_rows, weight_probe), ('gy', 'gx'))  482 us
    another operation x2, loops' own time, local(): lax.scan(visit, initial, (centres[:, 0], centres[:, 1], measured_all))  92.6 us
    dynamic_update_slice x48, local copies, waits for them, and re-layouts, visit(): lax.dynamic_update_slice(grad_obj, before + stacked, (zero_index, row_at,...  82.3 us
    dot_general x48, matrix products, transform(): jnp.einsum('crmq,cqdk->drmk', halfway, right_op, preferred_element_type=j...  54.9 us
    add x48, other arithmetic, visit(): return ((grad_obj, grad_probe + g_probe, weight_probe + w_probe), None)  53.1 us
    sub x24, other arithmetic, position_terms(): shrink = 1.0 - measured / jnp.sqrt(intensity + SOFT_FLOOR)  35.3 us
    while x312, local copies, waits for them, and re-layouts  34.1 us
    dynamic_slice x48, local copies, waits for them, and re-layouts, local(): lax.scan(visit, initial, (centres[:, 0], centres[:, 1], measured_all))  31.2 us
  transfers between devices with their start and end apart: 19, of which 12 were waited for; matrix products, arithmetic and copies ran while one was open for 1% of the time, Pallas kernels for 0%

profile of v1, /device:TPU:16, one launch (start us, length us, event | category | flops | bytes accessed | tf_op | source)
XLA Modules:
  0.0 1071.6 jit_solution(2636483579199690247)
XLA Ops:
  9.0 14.5 %all-to-all-start = ((f32[256,2,4,128]{3,2,1,0:T(4,128)}), f32[256,2,4,128]{3,2,1,0:T(4,128)S(1)}, u32[]{:S(2)}, u32[]{:S(2)}) async-start(f32[256,2,4,128]{3,2,1,0:T(4,128)} %stack.80), calls=%async_computation | async-start | bytes 2097152 | tf_op jit(solution)/shard_map/all_to_all | solution.py:109
  23.6 3.6 collective-permute-start
  27.2 5.8 collective-permute-start.1
  35.9 15.2 %collective-permute-done = f32[2,64,64]{1,2,0:T(8,128)S(1)} collective-permute-done((f32[2,64,64]{1,2,0:T(8,128)S(1)}, f32[2,64,64]{1,2,0:T(8,128)S(1)}, u32[]{:S(2)}, u32[]{:S(2)}) %collective-permute-start) | collective-permute-done | bytes 32800 | tf_op jit(solution)/shard_map/ppermute | solution.py:27
  54.5 3.5 collective-permute-done.3
  61.7 225.8 %while.38 = (s32[]{:T(128)}, f32[3,192,192]{2,1,0:T(8,128)}, f32[2,128,8,128]{1,3,0,2:T(8,128)}, f32[128,128]{0,1:T(8,128)}, s32[12]{0:T(128)S(1)}, /*index=5*/s...) while((s32[]{:T(128)}, f32[3,192,192]{2,1,0:T(8,128)}, ...), condition=%wide.region_5.6_spmd.clone, body=%wide.region_1.5_spmd.clone.sunk | while | flops 543391744 | bytes 25559488 | solution.py:146
  76.6 3.7 dynamic_update_slice.10
  95.4 3.8 dynamic_update_slice.10
  114.1 3.9 dynamic_update_slice.10
  133.1 3.8 dynamic_update_slice.10
  151.8 3.7 dynamic_update_slice.10
  170.6 3.9 dynamic_update_slice.10
  189.5 3.8 dynamic_update_slice.10
  208.3 3.8 dynamic_update_slice.10
  227.1 3.9 dynamic_update_slice.10
  246.0 3.7 dynamic_update_slice.10
  264.7 3.9 dynamic_update_slice.10
  283.6 3.9 dynamic_update_slice.10
  290.6 7.5 collective-permute-start.5
  302.3 4.3 collective-permute-start.6
  309.3 2.8 collective-permute-done.7
  314.9 7.5 collective-permute-start.9
  324.4 4.2 collective-permute-start.10
  330.1 2.7 collective-permute-done.11
  333.7 237.3 %all-reduce.7.cloned.1.call-done = (f32[2,1024,128]{2,1,0:T(8,128)}, f32[128,128]{0,1:T(8,128)}) async-done(((f32[2,1024,128]{2,1,0:T(8,128)}, f32[128,128]{0,1:T(8,128)}), (f32[2,1024,128]{2,1,0:T(8,128)}, f32[128,128]{0,1:T(8,128)})) %all-reduce.7.cloned.1.call-update) | async-done | bytes 1114128 | tf_op jit(solution)/shard_map/psum | solution.py:152
  575.4 220.6 %while.39 = (s32[]{:T(128)}, f32[3,192,192]{2,1,0:T(8,128)}, f32[2,128,8,128]{1,3,0,2:T(8,128)}, f32[128,128]{0,1:T(8,128)}, s32[12]{0:T(128)S(1)}, /*index=5*/s...) while((s32[]{:T(128)}, f32[3,192,192]{2,1,0:T(8,128)}, ...), condition=%wide.region_13.14_spmd.clone, body=%wide.region_9.13_spmd.clone.sunk | while | flops 543391744 | bytes 21627380 | solution.py:146
  589.0 2.7 dynamic_update_slice.11
  603.8 2.4 maximum_add_fusion.11
  607.4 2.8 dynamic_update_slice.11
  622.3 2.4 maximum_add_fusion.11
  625.9 2.8 dynamic_update_slice.11
  640.8 2.4 maximum_add_fusion.11
  644.4 2.8 dynamic_update_slice.11
  659.3 2.4 maximum_add_fusion.11
  662.9 2.7 dynamic_update_slice.11
  677.7 2.4 maximum_add_fusion.11
  681.3 2.8 dynamic_update_slice.11
  699.9 2.8 dynamic_update_slice.11
  718.4 2.8 dynamic_update_slice.11
  733.2 2.4 maximum_add_fusion.11
  736.8 2.8 dynamic_update_slice.11
  755.4 2.7 dynamic_update_slice.11
  773.8 2.9 dynamic_update_slice.11
  792.3 2.8 dynamic_update_slice.11
  799.0 7.5 collective-permute-start.13
  806.5 2.5 copy.134
  813.4 3.0 collective-permute-done.15
  817.9 244.5 %all-reduce.5.cloned.1.call-done = (f32[2,1024,128]{2,1,0:T(8,128)}, f32[128,128]{0,1:T(8,128)}) async-done(((f32[2,1024,128]{2,1,0:T(8,128)}, f32[128,128]{0,1:T(8,128)}), (f32[2,1024,128]{2,1,0:T(8,128)}, f32[128,128]{0,1:T(8,128)})) %all-reduce.5.cloned.1.call-update) | async-done | bytes 1114128 | tf_op jit(solution)/shard_map/psum | solution.py:152
  (752 shorter events, 304.3 us)
Async XLA Ops:
  9.0 14.6 %copy-start.19 = (f32[2,64,64]{2,1,0:T(8,128)S(1)}, f32[2,64,64]{2,1,0:T(8,128)}, u32[]{:S(2)}) copy-start(f32[2,64,64]{2,1,0:T(8,128)} %param.24) | copy-start | bytes 98308
  9.0 49.9 %all-to-all-start = ((f32[256,2,4,128]{3,2,1,0:T(4,128)}), f32[256,2,4,128]{3,2,1,0:T(4,128)S(1)}, u32[]{:S(2)}, u32[]{:S(2)}) async-start(f32[256,2,4,128]{3,2,1,0:T(4,128)} %stack.80), calls=%async_computation | async-start | bytes 2097152 | tf_op jit(solution)/shard_map/all_to_all | solution.py:109
  23.5 547.5 %all-reduce.7.cloned.1.call-start = ((), (), s32[]{:S(2)}) async-start(), calls=%async_computation.2 | async-start | bytes 2228224 | tf_op jit(solution)/shard_map/psum | solution.py:152
  23.6 27.5 %collective-permute-start = (f32[2,64,64]{1,2,0:T(8,128)S(1)}, f32[2,64,64]{1,2,0:T(8,128)S(1)}, u32[]{:S(2)}, u32[]{:S(2)}) collective-permute-start(f32[2,64,64]{1,2,0:T(8,128)S(1)} %copy.113), channel_id=1, source_target_pairs={{0,1},{1,2},{2,3},{3,4},{4,5},{5,6},{6,7},{7,8},{8,9},{9,10},{10,1... | collective-permute-start | bytes 98312 | tf_op jit(solution)/shard_map/ppermute | solution.py:27
  27.2 23.9 %collective-permute-start.1 = (f32[2,64,64]{1,2,0:T(8,128)S(1)}, f32[2,64,64]{1,2,0:T(8,128)S(1)}, u32[]{:S(2)}, u32[]{:S(2)}) collective-permute-start(f32[2,64,64]{1,2,0:T(8,128)S(1)} %copy.113), channel_id=1, source_target_pairs={{1,0},{2,1},{3,2},{4,3},{5,4},{6,5},{7,6},{8,7},{9,8},{10,9},{11,1... | collective-permute-start | bytes 98312 | tf_op jit(solution)/shard_map/ppermute | solution.py:28
  51.2 3.3 collective-permute-start.2
  52.5 5.5 collective-permute-start.3
  74.1 6.3 copy-start.1
  92.8 6.3 copy-start.1
  111.6 6.5 copy-start.1
  130.5 6.3 copy-start.1
  149.3 6.3 copy-start.1
  168.0 6.5 copy-start.1
  186.9 6.4 copy-start.1
  205.8 6.3 copy-start.1
  224.6 6.5 copy-start.1
  243.5 6.2 copy-start.1
  262.1 6.5 copy-start.1
  281.1 6.5 copy-start.1
  287.5 20.4 %copy-start.2 = (f32[2,128,8,128]{1,3,0,2:T(8,128)S(1)}, f32[2,128,8,128]{1,3,0,2:T(8,128)}, u32[]{:S(2)}) copy-start(f32[2,128,8,128]{1,3,0,2:T(8,128)} %get-tuple-element.247) | copy-start | bytes 3145732
  288.7 11.2 %collective-permute-start.4 = (f32[3,64,192]{2,1,0:T(8,128)S(1)}, f32[3,64,192]{2,1,0:T(8,128)S(1)}, u32[]{:S(2)}, u32[]{:S(2)}) collective-permute-start(f32[3,64,192]{2,1,0:T(8,128)S(1)} %get-tuple-element.593), channel_id=1, source_target_pairs={{0,1},{1,2},{2,3},{3,4},{4,5},{5,6},{6,7},{7,8},{8,9},{9,10},{10,1... | collective-permute-start | bytes 442376 | tf_op jit(solution)/shard_map/ppermute | solution.py:17
  290.6 10.7 collective-permute-start.5
  302.3 7.0 collective-permute-start.6
  306.6 5.5 collective-permute-start.7
  309.3 753.2 %all-reduce.5.cloned.1.call-start = ((), (), s32[]{:S(2)}) async-start(), calls=%async_computation.1 | async-start | bytes 2228224 | tf_op jit(solution)/shard_map/psum | solution.py:152
  312.2 259.7 %copy-start.4 = (f32[2,256,4,128]{3,2,1,0:T(4,128)S(1)}, f32[2,256,4,128]{3,2,1,0:T(4,128)}, u32[]{:S(2)}) copy-start(f32[2,256,4,128]{3,2,1,0:T(4,128)} %copy-done.3) | copy-start | bytes 3145732
  313.0 19.8 %copy-start.15 = (f32[2,64,64]{2,1,0:T(8,128)}, f32[2,64,64]{2,1,0:T(8,128)S(1)}, u32[]{:S(2)}) copy-start(f32[2,64,64]{2,1,0:T(8,128)S(1)} %fusion.67) | copy-start | bytes 98308
  313.0 9.8 collective-permute-start.8
  314.9 9.4 collective-permute-start.9
  324.4 5.7 collective-permute-start.10
  328.5 4.2 collective-permute-start.11
  589.0 2.7 copy-start.13
  607.4 2.8 copy-start.13
  625.9 2.8 copy-start.13
  644.4 2.8 copy-start.13
  662.9 2.7 copy-start.13
  681.3 2.9 copy-start.13
  699.9 2.8 copy-start.13
  718.4 2.8 copy-start.13
  736.8 2.8 copy-start.13
  755.3 2.7 copy-start.13
  773.7 2.9 copy-start.13
  792.3 2.8 copy-start.13
  797.0 12.0 %collective-permute-start.12 = (f32[3,64,192]{2,1,0:T(8,128)S(1)}, f32[3,64,192]{2,1,0:T(8,128)S(1)}, u32[]{:S(2)}, u32[]{:S(2)}) collective-permute-start(f32[3,64,192]{2,1,0:T(8,128)S(1)} %get-tuple-element.591), channel_id=1, source_target_pairs={{0,1},{1,2},{2,3},{3,4},{4,5},{5,6},{6,7},{7,8},{8,9},{9,10},{10,1... | collective-permute-start | bytes 442376 | tf_op jit(solution)/shard_map/ppermute | solution.py:17
  799.0 10.7 collective-permute-start.13
  810.6 2.6 copy-start.18
  810.7 2.7 collective-permute-start.14
  812.0 4.4 collective-permute-start.15
  (125 other events, 129.0 us)
Sparse Core Ops, SparseCore 0:
  309.4 261.5 all-reduce.6
  809.2 253.2 all-reduce.4
